TPU v7x, 32 devices: a whole 2x2x4 slice. The times are simulated.
32 devices in a mesh: dp: 8 (over z, y), ctx: 4 (over x, core).
Axes of the slice: x: 2, y: 2, z: 4, core: 2. Of those that a mesh axis runs over, the one named last changes fastest.
Arguments:
- tokens: bfloat16 [32768, 768], P(('dp', 'ctx')), may hold values from -6 to 6
- out_grad: bfloat16 [32768, 768], P(('dp', 'ctx')), may hold values from -6 to 6
- positions: int32 [32768], P(('dp', 'ctx')), may hold values from -1 to 2047, as said below
- master: float32 [55392, 128], P(('dp', 'ctx'))
- first_moment: float32 [55392, 128], P(('dp', 'ctx'))
- second_moment: float32 [55392, 128], P(('dp', 'ctx'))
- step_count: int32 [1], replicated, may hold values from 2 to 20
Outputs:
- layer_out: bfloat16 [32768, 768], P(('dp', 'ctx'))
- input_grad: float32 [32768, 768], P(('dp', 'ctx'))
- new_master: float32 [55392, 128], P(('dp', 'ctx'))
- new_first: float32 [55392, 128], P(('dp', 'ctx'))
- new_second: float32 [55392, 128], P(('dp', 'ctx'))
- weight_copy: bfloat16 [55392, 128], P(('dp', 'ctx'))
Inputs may be any that keep to these rules, and one draw needn't show every extreme that they name: `positions`: rows form blocks of 4096, one per index of dp. In a block, sequences of 1024 or 2048 rows start at multiples of 1024 from the block's start, each row holding its place in its sequence (0, 1, 2, ...); a block's first row holds 0, and the rows after its last sequence hold -1.
All inputs are finite; a program needn't handle non-finite values.
Results may differ from a plain program's by a relative error of at most 0.015.
The roundings to bfloat16 on the way count: a program that leaves them out, or rounds other values in their place, can miss the bound.
Values may be sent and summed in bfloat16 or wider, within the bound.
No kernel may reach another device: no remote copies, remote signals or barrier semaphores. Data moves between devices by JAX's collectives and lax.ppermute only.
A program may use at most 448 MiB of HBM per device.

v0:
```python
import jax
import jax.numpy as jnp
from jax import lax
from jax.sharding import PartitionSpec as P

D = 768
HEADS = 12
HEAD_DIM = 64
FF = 3072
SEQ_MIN = 1024
norm_eps = 1e-06


def from_behind(block, axis, distance):
    devices = range(lax.axis_size(axis))
    route = [(i - distance, i) for i in devices if i - distance in devices]
    return lax.ppermute(block, axis, route)


def unpack(flat):
    values = flat.reshape(-1)
    square_size = D * D
    wide_size = D * FF
    in_weight = jnp.concatenate(
        [
            values[0:square_size].reshape(D, D),
            values[square_size : 2 * square_size].reshape(D, D),
            values[2 * square_size : 3 * square_size].reshape(D, D),
        ],
        1,
    )
    out_weight = values[3 * square_size : 4 * square_size].reshape(D, D)
    up_weight = values[4 * square_size : 4 * square_size + wide_size].reshape(D, FF)
    down_weight = values[4 * square_size + wide_size : 4 * square_size + 2 * wide_size].reshape(
        FF, D
    )
    small_start = 4 * square_size + 2 * wide_size
    gain_first = values[small_start : small_start + D].astype(jnp.float32)
    gain_second = values[small_start + D : small_start + 2 * D].astype(jnp.float32)
    conv_taps = (
        values[small_start + 2 * D : small_start + 11 * D].reshape(3, 3 * D).astype(jnp.float32)
    )
    return (in_weight, out_weight, up_weight, down_weight, gain_first, gain_second, conv_taps)


def normalize(values, gain):
    factor = lax.rsqrt(jnp.mean(values * values, axis=-1, keepdims=True) + norm_eps)
    scaled = values * factor
    return (scaled, factor, scaled * gain)


def norm_back(grad_in, scaled, factor, gain):
    weighted = grad_in * gain
    inner_mean = jnp.mean(weighted * scaled, axis=-1, keepdims=True)
    return (factor * (weighted - scaled * inner_mean), jnp.sum(grad_in * scaled, axis=0))


def masked_scores(query_part, key_heads, query_rows, lowest_part, key_index):
    scores = (
        jnp.einsum("qhd,khd->hqk", query_part, key_heads, preferred_element_type=jnp.float32)
        * 0.125
    )
    allowed = (key_index[None, :] <= query_rows[:, None]) & (
        key_index[None, :] >= lowest_part[:, None]
    )
    return jnp.where(allowed[None], scores, -1e30)


def adam_update(master, moment_one, moment_two, gradient, step_count, row_start):
    row_index = row_start + jnp.arange(master.shape[0], dtype=jnp.int32)
    matrix_rows = (4 * D * D + 2 * D * FF) // 128
    out_first = 3 * D * D // 128
    out_last = 4 * D * D // 128
    is_matrix = (row_index < matrix_rows)[:, None]
    is_out = ((row_index >= out_first) & (row_index < out_last))[:, None]
    step_rate = jnp.where(is_matrix, jnp.where(is_out, 0.5, 0.1), 1.0)
    decay_rate = jnp.where(is_matrix, 0.1, 0.0)
    step_value = step_count[0].astype(jnp.float32)
    new_one = 0.9 * moment_one + 0.1 * gradient
    new_two = 0.999 * moment_two + 0.001 * gradient * gradient
    corr_first = 1.0 - jnp.power(0.9, step_value)
    corr_second = 1.0 - jnp.power(0.999, step_value)
    new_weights = master - step_rate * (
        new_one / corr_first / (jnp.sqrt(new_two / corr_second) + 1e-08) + decay_rate * master
    )
    return (new_weights, new_one, new_two)


def shards(tokens, out_grad, positions, master, first_moment, second_moment, step_count):
    rows_here = tokens.shape[0]
    span_rows = min(512, rows_here)
    span_count = rows_here // span_rows
    ctx_count = lax.axis_size("ctx")
    reach_back = min(ctx_count - 1, max(1, 2 * SEQ_MIN // rows_here - 1))
    ctx_place = lax.axis_index("ctx")
    triple_width = 3 * D
    shard_low = master.astype(jnp.bfloat16)
    gathered = lax.all_gather(shard_low, ("dp", "ctx"), axis=0, tiled=True)
    in_weight, out_weight, up_weight, down_weight, gain_first, gain_second, conv_taps = unpack(
        gathered
    )
    inputs = tokens.astype(jnp.float32)
    scaled_one, factor_one, normed_one = normalize(inputs, gain_first)
    normed_low = normed_one.astype(jnp.bfloat16)
    projected = jnp.dot(normed_low, in_weight, preferred_element_type=jnp.float32).astype(
        jnp.bfloat16
    )
    rim_rows = from_behind(projected[rows_here - 2 :], "ctx", 1)
    extended = jnp.concatenate([rim_rows, projected], 0).astype(jnp.float32)
    after_one = (positions >= 1).astype(jnp.float32)[:, None]
    after_two = (positions >= 2).astype(jnp.float32)[:, None]
    mixed_full = (
        conv_taps[0] * extended[2:]
        + after_one * conv_taps[1] * extended[1:-1]
        + after_two * conv_taps[2] * extended[:-2]
    )
    mixed_low = mixed_full.astype(jnp.bfloat16)
    query_heads = mixed_low[:, :D].reshape(rows_here, HEADS, HEAD_DIM)
    own_pairs = mixed_low[:, D:]
    earlier = [from_behind(own_pairs, "ctx", 1)]
    key_values = jnp.concatenate(earlier + [own_pairs], 0)
    key_heads = key_values[:, :D].reshape(-1, HEADS, HEAD_DIM)
    value_heads = key_values[:, D:].reshape(-1, HEADS, HEAD_DIM)
    key_index = (ctx_place - reach_back) * rows_here + jnp.arange(
        key_values.shape[0], dtype=jnp.int32
    )
    query_index = ctx_place * rows_here + jnp.arange(rows_here, dtype=jnp.int32)
    lowest = query_index - jnp.maximum(positions, 0)
    attended = []
    log_totals = []
    for span_at in range(span_count):
        rows_part = slice(span_at * span_rows, (span_at + 1) * span_rows)
        scores = masked_scores(
            query_heads[rows_part], key_heads, query_index[rows_part], lowest[rows_part], key_index
        )
        peak_score = jnp.max(scores, axis=-1, keepdims=True)
        raised = jnp.exp(scores - peak_score)
        total_sum = jnp.sum(raised, axis=-1, keepdims=True)
        probs_low = (raised / total_sum).astype(jnp.bfloat16)
        span_out = jnp.einsum(
            "hqk,khd->qhd", probs_low, value_heads, preferred_element_type=jnp.float32
        )
        attended.append(span_out.reshape(span_rows, D))
        log_totals.append(peak_score + jnp.log(total_sum))
    attn_low = jnp.concatenate(attended, 0).astype(jnp.bfloat16)
    hidden = inputs + jnp.dot(attn_low, out_weight, preferred_element_type=jnp.float32)
    scaled_two, factor_two, normed_two = normalize(hidden, gain_second)
    second_low = normed_two.astype(jnp.bfloat16)
    before = jnp.dot(second_low, up_weight, preferred_element_type=jnp.float32)
    active = jnp.maximum(before, 0.0)
    squared_low = (active * active).astype(jnp.bfloat16)
    layer_out = (
        hidden + jnp.dot(squared_low, down_weight, preferred_element_type=jnp.float32)
    ).astype(jnp.bfloat16)
    regathered = lax.all_gather(shard_low, ("dp", "ctx"), axis=0, tiled=True)
    in_weight, out_weight, up_weight, down_weight, gain_first, gain_second, conv_taps = unpack(
        regathered
    )
    fetched = [from_behind(own_pairs, "ctx", 1)]
    key_values = jnp.concatenate(fetched + [own_pairs], 0)
    key_heads = key_values[:, :D].reshape(-1, HEADS, HEAD_DIM)
    value_heads = key_values[:, D:].reshape(-1, HEADS, HEAD_DIM)
    grad_out = out_grad.astype(jnp.float32) * (positions >= 0).astype(jnp.float32)[:, None]
    grad_low = grad_out.astype(jnp.bfloat16)
    grad_down = jnp.einsum("tf,td->fd", squared_low, grad_low, preferred_element_type=jnp.float32)
    grad_squared = jnp.einsum(
        "td,fd->tf", grad_low, down_weight, preferred_element_type=jnp.float32
    )
    grad_before = (grad_squared * 2.0 * active).astype(jnp.bfloat16)
    grad_up = jnp.einsum("td,tf->df", second_low, grad_before, preferred_element_type=jnp.float32)
    grad_normed_two = jnp.einsum(
        "tf,df->td", grad_before, up_weight, preferred_element_type=jnp.float32
    )
    back_two, grad_gain_two = norm_back(grad_normed_two, scaled_two, factor_two, gain_second)
    grad_hidden = grad_out + back_two
    hidden_low = grad_hidden.astype(jnp.bfloat16)
    grad_outw = jnp.einsum("td,te->de", attn_low, hidden_low, preferred_element_type=jnp.float32)
    grad_attended = jnp.einsum(
        "te,de->td", hidden_low, out_weight, preferred_element_type=jnp.float32
    ).astype(jnp.bfloat16)
    grad_heads = grad_attended.reshape(rows_here, HEADS, HEAD_DIM)
    grad_query_parts = []
    grad_keys = jnp.zeros(key_heads.shape, jnp.float32)
    grad_values = jnp.zeros(value_heads.shape, jnp.float32)
    for span_at in range(span_count):
        rows_part = slice(span_at * span_rows, (span_at + 1) * span_rows)
        scores = masked_scores(
            query_heads[rows_part], key_heads, query_index[rows_part], lowest[rows_part], key_index
        )
        probs_full = jnp.exp(scores - log_totals[span_at])
        probs_low = probs_full.astype(jnp.bfloat16)
        grad_probs = jnp.einsum(
            "qhd,khd->hqk", grad_heads[rows_part], value_heads, preferred_element_type=jnp.float32
        )
        inner_sum = jnp.sum(probs_full * grad_probs, axis=-1, keepdims=True)
        grad_scores = (probs_full * (grad_probs - inner_sum)).astype(jnp.bfloat16)
        grad_query_parts.append(
            jnp.einsum("hqk,khd->qhd", grad_scores, key_heads, preferred_element_type=jnp.float32)
            * 0.125
        )
        grad_keys = (
            grad_keys
            + jnp.einsum(
                "hqk,qhd->khd",
                grad_scores,
                query_heads[rows_part],
                preferred_element_type=jnp.float32,
            )
            * 0.125
        )
        grad_values = grad_values + jnp.einsum(
            "hqk,qhd->khd", probs_low, grad_heads[rows_part], preferred_element_type=jnp.float32
        )
    grad_query = jnp.concatenate(grad_query_parts, 0).reshape(rows_here, D)
    grad_pairs = jnp.concatenate([grad_keys.reshape(-1, D), grad_values.reshape(-1, D)], 1)
    own_grad = grad_pairs[reach_back * rows_here :]
    piece_rows = grad_pairs[(reach_back - 1) * rows_here : (reach_back - 1 + 1) * rows_here]
    own_grad = own_grad + from_behind(piece_rows.astype(jnp.bfloat16), "ctx", -1).astype(
        piece_rows.dtype
    )
    grad_mixed = jnp.concatenate([grad_query, own_grad], 1)
    lead_rows = jnp.stack(
        [
            conv_taps[2] * after_two[0] * grad_mixed[0],
            conv_taps[1] * after_one[0] * grad_mixed[0]
            + conv_taps[2] * after_two[1] * grad_mixed[1],
        ]
    )
    tail_rows = from_behind(lead_rows, "ctx", -1)
    grad_projected = (
        conv_taps[0] * grad_mixed
        + jnp.concatenate(
            [
                conv_taps[1] * after_one[1:] * grad_mixed[1:],
                jnp.zeros((1, triple_width), jnp.float32),
            ],
            0,
        )
        + jnp.concatenate(
            [
                conv_taps[2] * after_two[2:] * grad_mixed[2:],
                jnp.zeros((2, triple_width), jnp.float32),
            ],
            0,
        )
        + jnp.concatenate([jnp.zeros((rows_here - 2, triple_width), jnp.float32), tail_rows], 0)
    )
    tap_grads = jnp.stack(
        [
            jnp.sum(grad_mixed * extended[2:], axis=0),
            jnp.sum(after_one * grad_mixed * extended[1:-1], axis=0),
            jnp.sum(after_two * grad_mixed * extended[:-2], axis=0),
        ]
    )
    projected_grad_low = grad_projected.astype(jnp.bfloat16)
    grad_inw = jnp.einsum(
        "td,te->de", normed_low, projected_grad_low, preferred_element_type=jnp.float32
    )
    grad_normed_one = jnp.einsum(
        "te,de->td", projected_grad_low, in_weight, preferred_element_type=jnp.float32
    )
    back_one, grad_gain_one = norm_back(grad_normed_one, scaled_one, factor_one, gain_first)
    input_grad = grad_hidden + back_one
    total_rows = gathered.shape[0]
    used_count = 4 * D * D + 2 * D * FF + 11 * D
    flat_grad = jnp.concatenate(
        [
            grad_inw[:, :D].reshape(-1),
            grad_inw[:, D : 2 * D].reshape(-1),
            grad_inw[:, 2 * D :].reshape(-1),
            grad_outw.reshape(-1),
            grad_up.reshape(-1),
            grad_down.reshape(-1),
            grad_gain_one,
            grad_gain_two,
            tap_grads.reshape(-1),
            jnp.zeros((total_rows * 128 - used_count,), jnp.float32),
        ]
    ).reshape(total_rows, 128)
    grad_shard = lax.psum_scatter(flat_grad, ("dp", "ctx"), scatter_dimension=0, tiled=True)
    row_start = lax.axis_index(("dp", "ctx")) * master.shape[0]
    new_weights, new_one, new_two = adam_update(
        master, first_moment, second_moment, grad_shard, step_count, row_start
    )
    return (layer_out, input_grad, new_weights, new_one, new_two, new_weights.astype(jnp.bfloat16))


def solution(mesh):
    return jax.shard_map(
        shards,
        mesh=mesh,
        in_specs=(
            P(("dp", "ctx"), None),
            P(("dp", "ctx"), None),
            P(("dp", "ctx")),
            P(("dp", "ctx"), None),
            P(("dp", "ctx"), None),
            P(("dp", "ctx"), None),
            P(),
        ),
        out_specs=(
            P(("dp", "ctx"), None),
            P(("dp", "ctx"), None),
            P(("dp", "ctx"), None),
            P(("dp", "ctx"), None),
            P(("dp", "ctx"), None),
            P(("dp", "ctx"), None),
        ),
        check_vma=False,
    )
```

profile of v0, /device:TPU:1, one launch (start us, length us, event | category | flops | bytes accessed | tf_op | source)
XLA Modules:
  0.0 1157.4 jit_solution(14164347562141519024)
XLA Ops:
  14.8 3.2 copy.59
  22.5 95.1 %all-gather.3.cloned.1.call-done = bf16[32,1731,128]{2,1,0:T(8,128)(2,1)} async-done(((bf16[1,1731,128]{2,1,0:T(8,128)(2,1)}), bf16[32,1731,128]{2,1,0:T(8,128)(2,1)}) %all-gather.3.cloned.1.call-update) | async-done | bytes 14180368 | tf_op jit(solution)/shard_map/all_gather | solution.py:98
  117.6 11.5 reshape.356
  131.1 4.2 fusion.78
  135.3 3.3 reshape.334
  138.7 3.4 reshape.333
  148.0 4.5 convolution_convert_fusion
  159.1 4.7 add_convert_fusion.1
  165.8 3.2 collective-permute-start.1
  170.3 3.9 fusion.77
  174.2 8.3 reshape.340
  184.4 9.2 reshape.341
  197.4 5.7 collective-permute-done.1
  203.1 5.1 pad_maximum_fusion.2
  208.2 3.2 copy.56
  211.4 5.4 copy.54
  216.8 21.5 %fusion.13 = (f32[12,512]{1,0:T(8,128)S(1)}, f32[12,512,2048]{2,1,0:T(8,128)}) fusion(pred[512,2048]{1,0:T(8,128)(4,1)} %get-tuple-element.61, bf16[512,12,64]{0,2,1:T(8,128)(2,1)} %bitcast.124, bf16[2048,12,64]{0,2,1:T(8,128)(2,1)S(1)} %bitcast.103), kind=kOutput, calls=%fused_computation.27 | convolution fusion | flops 1648355328 | bytes 55336960 | tf_op jit(solution)/shard_map/qhd,khd->hqk/dot_general | solution.py:60
  238.4 22.9 %fusion.1 = f32[12,512]{1,0:T(8,128)S(1)} fusion(f32[12,512]{1,0:T(8,128)S(1)} %get-tuple-element.74, f32[12,512,2048]{2,1,0:T(8,128)} %get-tuple-element.75, pred[512,2048]{1,0:T(8,128)(4,1)} %get-tuple-element.61), kind=kLoop, calls=%fused_computation.12 | loop fusion | flops 50325504 | bytes 51429376 | tf_op jit(solution)/shard_map/reduce_sum | solution.py:138
  261.9 21.9 %fusion.40 = bf16[12,64,512]{2,1,0:T(8,128)(2,1)} fusion(bf16[2048,12,64]{0,2,1:T(8,128)(2,1)} %bitcast.114, f32[12,512]{1,0:T(8,128)S(1)} %fusion.1, f32[12,512]{1,0:T(8,128)S(1)} %get-tuple-element.74, f32[12,512,2048]{2,1,0:T(8,128)} %get-tuple-element.75, pred[512,2048]{1,0:T(8,128)(4,1)S(1)} %copy-done.4), kind=kOutput, calls=%fused_computation.90 | convolution fusion | flops 1673920512 | bytes 55361536 | tf_op jit(solution)/shard_map/hqk,khd->qhd/dot_general | solution.py:140
  283.8 21.5 %fusion.14 = (f32[12,512]{1,0:T(8,128)S(1)}, f32[12,512,2048]{2,1,0:T(8,128)}) fusion(pred[512,2048]{1,0:T(8,128)(4,1)} %get-tuple-element.62, bf16[512,12,64]{0,2,1:T(8,128)(2,1)} %bitcast.122, bf16[2048,12,64]{0,2,1:T(8,128)(2,1)S(1)} %bitcast.104), kind=kOutput, calls=%fused_computation.28 | convolution fusion | flops 1648355328 | bytes 55336960 | tf_op jit(solution)/shard_map/qhd,khd->hqk/dot_general | solution.py:60
  305.3 22.9 %fusion.2 = f32[12,512]{1,0:T(8,128)S(1)} fusion(f32[12,512]{1,0:T(8,128)S(1)} %get-tuple-element.72, f32[12,512,2048]{2,1,0:T(8,128)} %get-tuple-element.73, pred[512,2048]{1,0:T(8,128)(4,1)} %get-tuple-element.62), kind=kLoop, calls=%fused_computation.13 | loop fusion | flops 50325504 | bytes 51429376 | tf_op jit(solution)/shard_map/reduce_sum | solution.py:138
  328.2 22.0 %fusion.39 = bf16[12,64,512]{2,1,0:T(8,128)(2,1)} fusion(bf16[2048,12,64]{0,2,1:T(8,128)(2,1)} %bitcast.115, f32[12,512]{1,0:T(8,128)S(1)} %fusion.2, f32[12,512]{1,0:T(8,128)S(1)} %get-tuple-element.72, f32[12,512,2048]{2,1,0:T(8,128)} %get-tuple-element.73, pred[512,2048]{1,0:T(8,128)(4,1)S(1)} %copy-done.3), kind=kOutput, calls=%fused_computation.89 | convolution fusion | flops 1673920512 | bytes 55361536 | tf_op jit(solution)/shard_map/hqk,khd->qhd/dot_general | solution.py:140
  353.5 8.6 fusion.73
  362.1 10.5 add_convert_fusion.2
  372.6 10.3 multiply_convert_fusion.2
  382.9 12.6 %fusion.38 = f32[3072,768]{1,0:T(8,128)} fusion(f32[1024,3072]{1,0:T(8,128)} %fusion.73, bf16[1024,768]{0,1:T(8,128)(2,1)S(1)} %copy-done.16, f32[1024]{0:T(1024)S(1)} %copy-done.43), kind=kOutput, calls=%fused_computation.85 | convolution fusion | flops 4843634688 | bytes 23597056 | tf_op jit(solution)/shard_map/tf,td->fd/dot_general | solution.py:165
  395.5 6.2 multiply_reduce_fusion.5
  401.7 7.7 convolution_bitcast_fusion
  415.8 22.9 %fusion.5 = f32[12,64,2048]{2,1,0:T(8,128)} fusion(bf16[512,12,64]{0,2,1:T(8,128)(2,1)S(1)} %bitcast.131, f32[12,512]{1,0:T(8,128)S(1)} %log_add_fusion, f32[12,512,2048]{2,1,0:T(8,128)} %get-tuple-element.73, pred[512,2048]{1,0:T(8,128)(4,1)S(1)} %copy-done.3), kind=kOutput, calls=%fused_computation.16 | convolution fusion | flops 1660944384 | bytes 58482688 | tf_op jit(solution)/shard_map/hqk,qhd->khd/dot_general | solution.py:211
  438.8 37.1 %multiply_reduce_fusion = (f32[12,512]{1,0:T(8,128)S(1)}, f32[12,512,2048]{2,1,0:T(8,128)}) fusion(f32[12,512]{1,0:T(8,128)S(1)} %log_add_fusion, f32[12,512,2048]{2,1,0:T(8,128)} %get-tuple-element.73, pred[512,2048]{1,0:T(8,128)(4,1)S(1)} %copy-done.3, bf16[512,12,64]{0,2,1:T(8,128)(2,1)S(1)} %bitcast.132, bf16[2048,12,64]{0,2,1:T(8,128)(2,1)} %bitcast.116), kind=kOutput, calls=%fused_computation.1 | convolution fusion | flops 1673521152 | bytes 105693184 | tf_op jit(solution)/shard_map/qhd,khd->hqk/dot_general | solution.py:192
  478.5 11.1 reshape.350
  489.6 9.5 copy.75
  499.1 3.2 reshape.348
  502.3 37.1 %multiply_reduce_fusion.1 = (f32[12,512]{1,0:T(8,128)S(1)}, f32[12,512,2048]{2,1,0:T(8,128)}) fusion(f32[12,512]{1,0:T(8,128)S(1)} %copy-done.21, f32[12,512,2048]{2,1,0:T(8,128)} %get-tuple-element.75, pred[512,2048]{1,0:T(8,128)(4,1)S(1)} %copy-done.5, bf16[512,12,64]{0,2,1:T(8,128)(2,1)S(1)} %bitcast.129, bf16[2048,12,64]{0,2,1:T(8,128)(2,1)} %bitcast.117), kind=kOutput, calls=%fused_computation.4 | convolution fusion | flops 1673521152 | bytes 105693184 | tf_op jit(solution)/shard_map/qhd,khd->hqk/dot_general | solution.py:192
  539.5 25.3 %fusion.26 = f32[12,64,2048]{2,1,0:T(8,128)} fusion(f32[12,64,2048]{2,1,0:T(8,128)} %fusion.5, bf16[512,12,64]{0,2,1:T(8,128)(2,1)S(1)} %bitcast.130, f32[12,512]{1,0:T(8,128)S(1)} %copy-done.21, f32[12,512,2048]{2,1,0:T(8,128)} %get-tuple-element.75, pred[512,2048]{1,0:T(8,128)(4,1)S(1)} %copy-done.5), kind=kOutput, calls=%fused_computation.65 | convolution fusion | flops 1662517248 | bytes 64774144 | tf_op jit(solution)/shard_map/hqk,qhd->khd/dot_general | solution.py:211
  564.8 6.6 copy.62
  571.4 40.6 %multiply_convert_fusion.1 = bf16[12,512,2048]{2,1,0:T(8,128)(2,1)} fusion(f32[12,512,2048]{2,1,0:T(8,128)} %get-tuple-element.80, f32[12,512]{1,0:T(8,128)S(1)} %get-tuple-element.79, f32[12,512]{1,0:T(8,128)S(1)} %copy-done.21, f32[12,512,2048]{2,1,0:T(8,128)} %get-tuple-element.75, pred[512,2048]{1,0:T(8,128)(4,1)S(1)} %copy-done.5), kind=kLoop, calls=%fused_computation.3 | loop fusion | flops 75497472 | bytes 126926848 | tf_op jit(solution)/shard_map/convert_element_type | solution.py:196
  612.0 15.4 %fusion.85 = f32[12,64,2048]{2,1,0:T(8,128)} fusion(bf16[512,12,64]{0,2,1:T(8,128)(2,1)S(1)} %bitcast.125, bf16[12,512,2048]{2,1,0:T(8,128)(2,1)} %multiply_convert_fusion.1), kind=kOutput, calls=%fused_computation.173 | convolution fusion | flops 1610612736 | bytes 32243712 | tf_op jit(solution)/shard_map/hqk,qhd->khd/dot_general | solution.py:203
  627.4 40.4 %multiply_convert_fusion = bf16[12,512,2048]{2,1,0:T(8,128)(2,1)} fusion(f32[12,512,2048]{2,1,0:T(8,128)} %get-tuple-element.82, f32[12,512]{1,0:T(8,128)S(1)} %get-tuple-element.81, f32[12,512]{1,0:T(8,128)S(1)} %log_add_fusion, f32[12,512,2048]{2,1,0:T(8,128)} %get-tuple-element.73, pred[512,2048]{1,0:T(8,128)(4,1)S(1)} %copy-done.3), kind=kLoop, calls=%fused_computation | loop fusion | flops 75497472 | bytes 126926848 | tf_op jit(solution)/shard_map/convert_element_type | solution.py:196
  667.8 17.2 %add_multiply_fusion = f32[12,64,2048]{2,1,0:T(8,128)} fusion(f32[12,64,2048]{2,1,0:T(8,128)} %fusion.85, bf16[512,12,64]{0,2,1:T(8,128)(2,1)S(1)} %bitcast.123, bf16[12,512,2048]{2,1,0:T(8,128)(2,1)} %multiply_convert_fusion), kind=kOutput, calls=%fused_computation.52 | convolution fusion | flops 1613758464 | bytes 38535168 | tf_op jit(solution)/shard_map/hqk,qhd->khd/dot_general | solution.py:203
  685.0 6.6 copy.61
  691.6 5.0 fusion.21
  698.5 13.7 %multiply_bitcast_fusion.1 = f32[512,12,64]{0,2,1:T(8,128)} fusion(bf16[2048,12,64]{0,2,1:T(8,128)(2,1)S(1)} %bitcast.105, bf16[12,512,2048]{2,1,0:T(8,128)(2,1)} %multiply_convert_fusion.1), kind=kOutput, calls=%fused_computation.88 | convolution fusion | flops 1611005952 | bytes 29884416 | tf_op jit(solution)/shard_map/hqk,khd->qhd/dot_general | solution.py:198
  712.2 13.7 %multiply_bitcast_fusion = f32[512,12,64]{0,2,1:T(8,128)} fusion(bf16[2048,12,64]{0,2,1:T(8,128)(2,1)S(1)} %bitcast.106, bf16[12,512,2048]{2,1,0:T(8,128)(2,1)} %multiply_convert_fusion), kind=kOutput, calls=%fused_computation.87 | convolution fusion | flops 1611005952 | bytes 29884416 | tf_op jit(solution)/shard_map/hqk,khd->qhd/dot_general | solution.py:198
  725.9 4.0 pad_maximum_fusion.3
  732.3 3.9 collective-permute-done.2
  736.2 4.2 fusion.20
  743.2 5.7 fusion.16
  748.9 4.6 fusion.18
  753.6 13.7 %multiply_reduce_fusion.4 = (f32[2304]{0:T(1024)S(1)}, f32[2304]{0:T(1024)S(1)}, f32[2304]{0:T(1024)S(1)}, bf16[1024,2304]{1,0:T(8,128)(2,1)}) fusion(f32[1026,2304]{1,0:T(8,128)S(1)} %bitcast.102, f32[1024,1536]{1,0:T(8,128)S(1)} %fusion.20, f32[1024,768]{1,0:T(8,128)S(1)} %copy.63, f32[1024]{0:T(1024)S(1)} %copy-done.31, f32[1024]{0:T(1024)S(1)} %copy-done.33, ...), kind=kLoop, calls=%fused_computation.43 | loop fusion | flops 33023232 | bytes 61377536 | tf_op jit(solution)/shard_map/reduce_sum | solution.py:250
  767.3 9.3 fusion.34
  776.6 6.0 fusion.47
  782.7 5.8 fusion.79
  788.4 3.2 reshape.347
  791.7 3.2 reshape.346
  796.5 3.4 constant_dynamic-update-slice_fusion.3
  799.9 4.1 constant_dynamic-update-slice_fusion.11
  807.8 4.9 constant_dynamic-update-slice_fusion.8
  814.2 3.8 constant_dynamic-update-slice_fusion.7
  823.2 307.1 %fusion = f32[1744,128]{1,0:T(8,128)S(1)} fusion(f32[55392,128]{1,0:T(8,128)} %bitcast.26), kind=kCustom, calls=%all-reduce-scatter | all-reduce-scatter fusion | flops 7143425 | bytes 29253632
  1131.0 4.4 collective-permute-start.4
  1135.4 5.2 fusion.33
  1140.7 3.6 copy.68
  1146.6 3.6 fusion.74
  (208 shorter events, 69.7 us)
Async XLA Ops:
  7.2 12.4 %copy-start.44 = (s32[1024]{0:T(1024)S(1)}, s32[1024]{0:T(1024)}, u32[]{:S(2)}) copy-start(s32[1024]{0:T(1024)} %param.9) | copy-start | bytes 12292
  7.2 110.4 %all-gather.3.cloned.1.call-start = ((), (), s32[]{:S(2)}) async-start(), calls=%async_computation | async-start | bytes 14665728 | tf_op jit(solution)/shard_map/all_gather | solution.py:98
  10.5 148.5 %copy-start.30 = (f32[1024]{0:T(1024)}, f32[1024]{0:T(1024)S(1)}, u32[]{:S(2)}) copy-start(f32[1024]{0:T(1024)S(1)} %get-tuple-element.66) | copy-start | bytes 12292
  10.5 148.5 %copy-start.32 = (f32[1024]{0:T(1024)}, f32[1024]{0:T(1024)S(1)}, u32[]{:S(2)}) copy-start(f32[1024]{0:T(1024)S(1)} %get-tuple-element.67) | copy-start | bytes 12292
  14.8 133.1 %copy-start.7 = (bf16[1024,768]{0,1:T(8,128)(2,1)}, bf16[1024,768]{0,1:T(8,128)(2,1)S(1)}, u32[]{:S(2)}) copy-start(bf16[1024,768]{0,1:T(8,128)(2,1)S(1)} %copy.53) | copy-start | bytes 4718596
  19.6 128.4 %copy-start.41 = (f32[1024]{0:T(1024)}, f32[1024]{0:T(1024)S(1)}, u32[]{:S(2)}) copy-start(f32[1024]{0:T(1024)S(1)} %add_rsqrt_fusion.1) | copy-start | bytes 12292
  130.4 17.6 %copy-start.39 = (f32[768]{0:T(1024)}, f32[768]{0:T(1024)S(1)}, u32[]{:S(2)}) copy-start(f32[768]{0:T(1024)S(1)} %get-tuple-element.38) | copy-start | bytes 9220
  147.9 4.5 copy-start.23
  152.5 5.6 collective-permute-start
  159.0 4.8 copy-start
  159.0 10.0 slice-start.3
  159.1 9.9 slice-start.4
  159.1 10.8 slice-start.5
  159.1 11.2 slice-start.6
  163.8 10.3 copy-start.6
  165.8 37.3 %collective-permute-start.1 = (bf16[1024,1536]{1,0:T(8,128)(2,1)}, bf16[1024,1536]{1,0:T(8,128)(2,1)}, u32[]{:S(2)}, u32[]{:S(2)}) collective-permute-start(bf16[1024,1536]{1,0:T(8,128)(2,1)} %slice.244), channel_id=1, source_target_pairs={{0,1},{1,2},{2,3},{4,5},{5,6},{6,7},{8,9},{9,10},{10,11},{12,13},{... | collective-permute-start | bytes 9437192 | tf_op jit(solution)/shard_map/ppermute | solution.py:17
  174.2 8.3 copy-start.18
  211.4 72.4 %copy-start.1 = (bf16[2048,768]{0,1:T(8,128)(2,1)}, bf16[2048,768]{0,1:T(8,128)(2,1)S(1)}, u32[]{:S(2)}) copy-start(bf16[2048,768]{0,1:T(8,128)(2,1)S(1)} %copy.56) | copy-start | bytes 9437188
  238.4 23.6 %copy-start.4 = (pred[512,2048]{1,0:T(8,128)(4,1)S(1)}, pred[512,2048]{1,0:T(8,128)(4,1)}, u32[]{:S(2)}) copy-start(pred[512,2048]{1,0:T(8,128)(4,1)} %get-tuple-element.61) | copy-start | bytes 3145732
  305.3 22.9 %copy-start.3 = (pred[512,2048]{1,0:T(8,128)(4,1)S(1)}, pred[512,2048]{1,0:T(8,128)(4,1)}, u32[]{:S(2)}) copy-start(pred[512,2048]{1,0:T(8,128)(4,1)} %get-tuple-element.62) | copy-start | bytes 3145732
  328.2 22.1 %copy-start.8 = (bf16[1024,768]{0,1:T(8,128)(2,1)S(1)}, bf16[1024,768]{0,1:T(8,128)(2,1)}, u32[]{:S(2)}) copy-start(bf16[1024,768]{0,1:T(8,128)(2,1)} %copy-done.7) | copy-start | bytes 4718596
  328.2 22.1 %copy-start.20 = (bf16[768,768]{1,0:T(8,128)(2,1)S(1)}, bf16[768,768]{1,0:T(8,128)(2,1)}, u32[]{:S(2)}) copy-start(bf16[768,768]{1,0:T(8,128)(2,1)} %reshape.339) | copy-start | bytes 3538948
  350.2 3.2 copy-start.22
  350.3 3.2 slice-start.14
  353.5 19.1 %slice-start.15 = ((s8[4718592]{0:T(1024)(128)(4,1)}), s8[4194304]{0:T(1024)(128)(4,1)S(1)}, s32[]{:S(2)}) async-start(s8[4718592]{0:T(1024)(128)(4,1)} %bitcast.127), calls=%async_computation.16 | async-start | bytes 8388608
  362.0 10.6 copy-start.16
  362.0 10.6 slice-start.16
  362.0 10.6 copy-start.43
  382.9 12.6 %copy-start.50 = (bf16[1024,3072]{1,0:T(8,128)(2,1)S(1)}, bf16[1024,3072]{1,0:T(8,128)(2,1)}, u32[]{:S(2)}) copy-start(bf16[1024,3072]{1,0:T(8,128)(2,1)} %multiply_convert_fusion.2) | copy-start | bytes 18874372
  410.4 5.3 copy-start.11
  489.6 12.7 %copy-start.5 = (pred[512,2048]{1,0:T(8,128)(4,1)S(1)}, pred[512,2048]{1,0:T(8,128)(4,1)}, u32[]{:S(2)}) copy-start(pred[512,2048]{1,0:T(8,128)(4,1)} %get-tuple-element.61) | copy-start | bytes 3145732
  489.6 12.7 %copy-start.21 = (f32[12,512]{1,0:T(8,128)S(1)}, f32[12,512]{1,0:T(8,128)}, u32[]{:S(2)}) copy-start(f32[12,512]{1,0:T(8,128)} %log_add_fusion.1) | copy-start | bytes 73732
  571.4 40.6 %copy-start.15 = (bf16[512,768]{0,1:T(8,128)(2,1)S(1)}, bf16[512,768]{0,1:T(8,128)(2,1)}, u32[]{:S(2)}) copy-start(bf16[512,768]{0,1:T(8,128)(2,1)} %copy.55) | copy-start | bytes 2359300
  627.4 40.4 %copy-start.14 = (bf16[512,768]{0,1:T(8,128)(2,1)S(1)}, bf16[512,768]{0,1:T(8,128)(2,1)}, u32[]{:S(2)}) copy-start(bf16[512,768]{0,1:T(8,128)(2,1)} %copy.57) | copy-start | bytes 2359300
  691.6 6.9 copy-start.2
  696.6 39.6 %collective-permute-start.2 = (bf16[1024,1536]{1,0:T(8,128)(2,1)}, bf16[1024,1536]{1,0:T(8,128)(2,1)}, u32[]{:S(2)}, u32[]{:S(2)}) collective-permute-start(bf16[1024,1536]{1,0:T(8,128)(2,1)} %fusion.21), channel_id=1, source_target_pairs={{1,0},{2,1},{3,2},{5,4},{6,5},{7,6},{9,8},{10,9},{11,10},{13,12},{... | collective-permute-start | bytes 9437192 | tf_op jit(solution)/shard_map/ppermute | solution.py:17
  732.3 8.2 copy-start.36
  741.2 7.7 copy-start.25
  741.2 7.7 copy-start.46
  741.2 12.3 %collective-permute-start.3 = (f32[2,2304]{1,0:T(2,128)S(1)}, f32[2,2304]{1,0:T(2,128)S(1)}, u32[]{:S(2)}, u32[]{:S(2)}) collective-permute-start(f32[2,2304]{1,0:T(2,128)S(1)} %pad_maximum_fusion.8), channel_id=1, source_target_pairs={{1,0},{2,1},{3,2},{5,4},{6,5},{7,6},{9,8},{10,9},{11,10},{13,12},{... | collective-permute-start | bytes 55304 | tf_op jit(solution)/shard_map/ppermute | solution.py:17
  743.2 10.3 slice-start
  743.2 10.3 slice-start.1
  748.9 4.6 slice-start.2
  748.9 4.6 copy-start.29
  748.9 4.6 copy-start.31
  748.9 4.6 copy-start.33
  753.5 13.8 %copy-start.9 = (bf16[1024,768]{0,1:T(8,128)(2,1)S(1)}, bf16[1024,768]{0,1:T(8,128)(2,1)}, u32[]{:S(2)}) copy-start(bf16[1024,768]{0,1:T(8,128)(2,1)} %copy-done.7) | copy-start | bytes 4718596
  753.5 13.8 %copy-start.40 = (f32[768]{0:T(1024)S(1)}, f32[768]{0:T(1024)}, u32[]{:S(2)}) copy-start(f32[768]{0:T(1024)} %copy-done.39) | copy-start | bytes 9220
  753.5 13.8 %copy-start.42 = (f32[1024]{0:T(1024)S(1)}, f32[1024]{0:T(1024)}, u32[]{:S(2)}) copy-start(f32[1024]{0:T(1024)} %copy-done.41) | copy-start | bytes 12292
  767.3 9.3 copy-start.17
  794.9 12.2 %slice-start.10 = ((s8[9437184]{0:T(1024)(128)(4,1)}), s8[1048576]{0:T(1024)(128)(4,1)S(1)}, s32[]{:S(2)}) async-start(s8[9437184]{0:T(1024)(128)(4,1)} %bitcast.111), calls=%async_computation.11 | async-start | bytes 2097152
  796.5 7.4 copy-start.13
  796.5 9.0 copy-start.12
  796.5 10.6 slice-start.11
  803.9 3.9 slice-start.12
  807.1 5.6 slice-start.7
  807.8 6.1 slice-start.8
  807.8 6.3 slice-start.9
  814.2 5.1 copy-start.47
  823.2 312.2 %copy-start.10 = (bf16[1024,768]{0,1:T(8,128)(2,1)S(1)}, bf16[1024,768]{0,1:T(8,128)(2,1)}, u32[]{:S(2)}) copy-start(bf16[1024,768]{0,1:T(8,128)(2,1)} %copy-done.7) | copy-start | bytes 4718596
  1131.0 13.3 %collective-permute-start.4 = (f32[403,128]{1,0:T(8,128)}, f32[403,128]{1,0:T(8,128)}, u32[]{:S(2)}, u32[]{:S(2)}) collective-permute-start(f32[403,128]{1,0:T(8,128)} %slice.268), channel_id=1, source_target_pairs={{0,1},{1,2},{2,3},{3,4},{4,5},{5,6},{6,7},{7,8},{8,9},{9,10},{10,1... | collective-permute-start | bytes 619016
  1140.7 5.9 copy-start.19
  1140.7 5.9 copy-start.37
  1140.7 5.9 copy-start.38
  (10 other events, 17.2 us)
Sparse Core Ops, SparseCore 0:
  11.5 106.0 all-gather.2
where the time goes:
time: 1170 us; the launch traced here: 1160 us
  matrix products  352 us (30%)
  blocking collectives  307 us (26%)
  other arithmetic  197 us (17%)
  local copies, waits for them, and re-layouts  166 us (14%)
  waiting for transfers between devices  105 us (9%)
  between operations  16.1 us (1%)
  starting transfers between devices  14.5 us (1%)
    unnamed x1, blocking collectives  307 us
    all_gather x1, waiting for transfers between devices, shards(): gathered = lax.all_gather(shard_low, ('dp', 'ctx'), axis=0, tiled=True)  95.1 us
    convert_element_type x2, other arithmetic, shards(): grad_scores = (probs_full * (grad_probs - inner_sum)).astype(jnp.bfloat16)  81 us
    dot_general x2, matrix products, shards(): jnp.einsum('qhd,khd->hqk', grad_heads[rows_part], value_heads, preferred_...  74.3 us
    unnamed x155, local copies, waits for them, and re-layouts  66.3 us
    dot_general x2, matrix products, shards(): jnp.einsum('hqk,qhd->khd', probs_low, grad_heads[rows_part], preferred_el...  48.3 us
    reduce_sum x2, other arithmetic, shards(): total_sum = jnp.sum(raised, axis=-1, keepdims=True)  45.8 us
    dot_general x2, matrix products, shards(): jnp.einsum('hqk,khd->qhd', probs_low, value_heads, preferred_element_type...  43.9 us
  transfers between devices with their start and end apart: 6, of which 3 were waited for; matrix products, arithmetic and copies ran while one was open for 8% of the time, Pallas kernels for 0%

commit v1 on v0

--- a/solution.py
+++ b/solution.py
@@ -95,7 +95,22 @@
     ctx_place = lax.axis_index("ctx")
     triple_width = 3 * D
     shard_low = master.astype(jnp.bfloat16)
-    gathered = lax.all_gather(shard_low, ("dp", "ctx"), axis=0, tiled=True)
+    ways, here, step = (
+        lax.axis_size(("dp", "ctx")),
+        lax.axis_index(("dp", "ctx")),
+        shard_low.shape[0],
+    )
+    line, have = (shard_low, 1)
+    while have < ways:
+        line = jnp.concatenate(
+            [
+                line,
+                lax.ppermute(line, ("dp", "ctx"), [(d, (d - have) % ways) for d in range(ways)]),
+            ],
+            axis=0,
+        )
+        have = 2 * have
+    gathered = jnp.roll(line, here * step, axis=0)
     in_weight, out_weight, up_weight, down_weight, gain_first, gain_second, conv_taps = unpack(
         gathered
     )

time: 1170 us -> 1760 us (1.50)
  waiting for transfers between devices: 105 us -> 445 us
  local copies, waits for them, and re-layouts: 166 us -> 396 us
    ppermute x0 -> x5, waiting for transfers between devices: none -> 445 us  [shards(): lax.ppermute(line, ('dp', 'ctx'), [(d, (d - have) % ways) for d in range(...]
    concatenate x1 -> x4, local copies, waits for them, and re-layouts: 1.35 us -> 175 us  [the longest x1 120 us: shards(): gathered = jnp.roll(line, here * step, axis=0)]
    all_gather x1, waiting for transfers between devices: 95.1 us -> 0.02 us  [shards(): regathered = lax.all_gather(shard_low, ('dp', 'ctx'), axis=0, tiled=True)]
    unnamed x155 -> x179, local copies, waits for them, and re-layouts: 66.3 us -> 72.7 us
  transfers between devices with their start and end apart: 6 -> 11, of which waited for: 3 -> 6; matrix products, arithmetic and copies ran while one was open for 8% -> 27% of each run, Pallas kernels for 0% -> 0%
where the time goes in v1:
time: 1760 us; the launch traced here: 1740 us
  waiting for transfers between devices  445 us (25%)
  local copies, waits for them, and re-layouts  396 us (22%)
  matrix products  353 us (20%)
  blocking collectives  302 us (17%)
  other arithmetic  203 us (12%)
  starting transfers between devices  27.8 us (2%)
    ppermute x5, waiting for transfers between devices, shards(): lax.ppermute(line, ('dp', 'ctx'), [(d, (d - have) % ways) for d in range(...  445 us
    unnamed x1, blocking collectives  302 us
    concatenate x1, local copies, waits for them, and re-layouts, shards(): gathered = jnp.roll(line, here * step, axis=0)  120 us
    convert_element_type x2, other arithmetic, shards(): grad_scores = (probs_full * (grad_probs - inner_sum)).astype(jnp.bfloat16)  82.2 us
    dot_general x2, matrix products, shards(): jnp.einsum('qhd,khd->hqk', grad_heads[rows_part], value_heads, preferred_...  75.5 us
    unnamed x179, local copies, waits for them, and re-layouts  72.7 us
    concatenate x3, local copies, waits for them, and re-layouts, shards(): jnp.concatenate([line, lax.ppermute(line, ('dp', 'ctx'), [(d, (d - have)...  54.8 us
    dot_general x2, matrix products, shards(): jnp.einsum('hqk,qhd->khd', probs_low, grad_heads[rows_part], preferred_el...  48.3 us
  transfers between devices with their start and end apart: 11, of which 6 were waited for; matrix products, arithmetic and copies ran while one was open for 27% of the time, Pallas kernels for 0%

profile of v1, /device:TPU:1, one launch (start us, length us, event | category | flops | bytes accessed | tf_op | source)
XLA Modules:
  0.0 1742.9 jit_solution(2095938853412040580)
XLA Ops:
  8.6 8.6 collective-permute-done
  17.3 8.8 collective-permute-start.1
  26.1 15.2 collective-permute-done.1
  41.2 8.8 concatenate.61
  51.9 38.1 %collective-permute-done.2 = bf16[6924,128]{1,0:T(8,128)(2,1)S(1)} collective-permute-done((bf16[6924,128]{1,0:T(8,128)(2,1)}, bf16[6924,128]{1,0:T(8,128)(2,1)S(1)}, u32[]{:S(2)}, u32[]{:S(2)}) %collective-permute-start.2) | collective-permute-done | bytes 1772576 | tf_op jit(solution)/shard_map/ppermute | solution.py:108
  91.2 16.1 concatenate.62
  108.6 77.1 %collective-permute-done.3 = bf16[13848,128]{1,0:T(8,128)(2,1)S(1)} collective-permute-done((bf16[13848,128]{1,0:T(8,128)(2,1)}, bf16[13848,128]{1,0:T(8,128)(2,1)S(1)}, u32[]{:S(2)}, u32[]{:S(2)}) %collective-permute-start.3) | collective-permute-done | bytes 3545120 | tf_op jit(solution)/shard_map/ppermute | solution.py:108
  185.8 29.9 %concatenate.63 = bf16[27696,128]{1,0:T(8,128)(2,1)} concatenate(bf16[1731,128]{1,0:T(8,128)(2,1)} %copy-done.12, bf16[1731,128]{1,0:T(8,128)(2,1)} %copy-done.14, bf16[3462,128]{1,0:T(8,128)(2,1)} %copy-done.11, bf16[6924,128]{1,0:T(8,128)(2,1)} %copy-done.9, bf16[13848,128]{1,0:T(8,128)(2,1)S(1)} %collective-permute-done.3), dimensions={0} | concatenate | bytes 14180352 | tf_op jit(solution)/shard_map/concatenate | solution.py:105
  226.4 305.7 %collective-permute-done.4 = bf16[27696,128]{1,0:T(8,128)(2,1)} collective-permute-done((bf16[27696,128]{1,0:T(8,128)(2,1)}, bf16[27696,128]{1,0:T(8,128)(2,1)}, u32[]{:S(2)}, u32[]{:S(2)}) %collective-permute-start.4) | collective-permute-done | bytes 7090208 | tf_op jit(solution)/shard_map/ppermute | solution.py:108
  532.0 119.8 %concatenate.64 = bf16[110784,128]{1,0:T(8,128)(2,1)} concatenate(bf16[1731,128]{1,0:T(8,128)(2,1)} %copy-done.12, bf16[1731,128]{1,0:T(8,128)(2,1)} %copy-done.14, bf16[3462,128]{1,0:T(8,128)(2,1)} %copy-done.11, bf16[6924,128]{1,0:T(8,128)(2,1)} %copy-done.9, bf16[13848,128]{1,0:T(8,128)(2,1)S(1)} %collective-permute-done.3, bf16[27696,128]{1,0:T(8,128)(2,1)} %collective-permute-done.4, ...), dimensions={0} | concatenate | bytes 56721408 | tf_op jit(solution)/shard_map/jit(_roll_dynamic)/concatenate | solution.py:113
  652.5 5.1 constant_dynamic-slice_fusion.5
  667.6 6.0 convolution_convert_fusion
  678.0 4.7 add_convert_fusion.1
  684.8 4.2 collective-permute-start.6
  697.7 9.4 constant_dynamic-slice_fusion
  707.1 8.2 reshape.389
  718.7 9.2 reshape.390
  735.1 6.1 pad_maximum_fusion.2
  744.4 5.4 copy.54
  749.9 21.5 %fusion.13 = (f32[12,512]{1,0:T(8,128)S(1)}, f32[12,512,2048]{2,1,0:T(8,128)}) fusion(pred[512,2048]{1,0:T(8,128)(4,1)} %get-tuple-element.72, bf16[512,12,64]{0,2,1:T(8,128)(2,1)} %bitcast.136, bf16[2048,12,64]{0,2,1:T(8,128)(2,1)S(1)} %bitcast.117), kind=kOutput, calls=%fused_computation.27 | convolution fusion | flops 1648355328 | bytes 55336960 | tf_op jit(solution)/shard_map/qhd,khd->hqk/dot_general | solution.py:60
  771.4 22.2 %fusion.1 = f32[12,512]{1,0:T(8,128)S(1)} fusion(f32[12,512]{1,0:T(8,128)S(1)} %get-tuple-element.85, f32[12,512,2048]{2,1,0:T(8,128)} %get-tuple-element.86, pred[512,2048]{1,0:T(8,128)(4,1)} %get-tuple-element.72), kind=kLoop, calls=%fused_computation.12 | loop fusion | flops 50325504 | bytes 51429376 | tf_op jit(solution)/shard_map/reduce_sum | solution.py:153
  793.6 21.5 %fusion.14 = (f32[12,512]{1,0:T(8,128)S(1)}, f32[12,512,2048]{2,1,0:T(8,128)}) fusion(pred[512,2048]{1,0:T(8,128)(4,1)} %get-tuple-element.73, bf16[512,12,64]{0,2,1:T(8,128)(2,1)} %bitcast.134, bf16[2048,12,64]{0,2,1:T(8,128)(2,1)S(1)} %bitcast.118), kind=kOutput, calls=%fused_computation.28 | convolution fusion | flops 1648355328 | bytes 55336960 | tf_op jit(solution)/shard_map/qhd,khd->hqk/dot_general | solution.py:60
  815.1 22.5 %fusion.2 = f32[12,512]{1,0:T(8,128)S(1)} fusion(f32[12,512]{1,0:T(8,128)S(1)} %get-tuple-element.83, f32[12,512,2048]{2,1,0:T(8,128)} %get-tuple-element.84, pred[512,2048]{1,0:T(8,128)(4,1)} %get-tuple-element.73), kind=kLoop, calls=%fused_computation.13 | loop fusion | flops 50325504 | bytes 51429376 | tf_op jit(solution)/shard_map/reduce_sum | solution.py:153
  837.7 21.0 %fusion.51 = bf16[12,64,512]{2,1,0:T(8,128)(2,1)} fusion(bf16[2048,12,64]{0,2,1:T(8,128)(2,1)S(1)} %bitcast.128, f32[12,512]{1,0:T(8,128)S(1)} %fusion.1, f32[12,512]{1,0:T(8,128)S(1)} %get-tuple-element.85, f32[12,512,2048]{2,1,0:T(8,128)} %get-tuple-element.86, pred[512,2048]{1,0:T(8,128)(4,1)S(1)} %copy-done.6), kind=kOutput, calls=%fused_computation.101 | convolution fusion | flops 1673920512 | bytes 55361536 | tf_op jit(solution)/shard_map/hqk,khd->qhd/dot_general | solution.py:155
  858.7 21.3 %fusion.50 = bf16[12,64,512]{2,1,0:T(8,128)(2,1)} fusion(bf16[2048,12,64]{0,2,1:T(8,128)(2,1)S(1)} %bitcast.129, f32[12,512]{1,0:T(8,128)S(1)} %fusion.2, f32[12,512]{1,0:T(8,128)S(1)} %get-tuple-element.83, f32[12,512,2048]{2,1,0:T(8,128)} %get-tuple-element.84, pred[512,2048]{1,0:T(8,128)(4,1)S(1)} %copy-done.4), kind=kOutput, calls=%fused_computation.100 | convolution fusion | flops 1673920512 | bytes 55361536 | tf_op jit(solution)/shard_map/hqk,khd->qhd/dot_general | solution.py:155
  883.3 5.4 fusion.90
  888.7 4.6 copy-done.19
  893.4 9.1 add_convert_fusion.2
  905.0 10.7 fusion.49
  915.8 10.8 reshape.405
  926.6 11.5 reshape.413
  939.4 4.6 fusion.94
  944.0 8.2 fusion.95
  952.2 8.2 reshape.392
  963.8 9.2 reshape.391
  973.0 10.0 multiply_convert_fusion.2
  983.0 9.9 multiply_reduce_fusion.5
  996.7 37.4 %multiply_reduce_fusion.1 = (f32[12,512]{1,0:T(8,128)S(1)}, f32[12,512,2048]{2,1,0:T(8,128)}) fusion(f32[12,512]{1,0:T(8,128)S(1)} %log_add_fusion.1, f32[12,512,2048]{2,1,0:T(8,128)} %get-tuple-element.86, pred[512,2048]{1,0:T(8,128)(4,1)S(1)} %copy-done.7, bf16[512,12,64]{0,2,1:T(8,128)(2,1)S(1)} %bitcast.139, bf16[2048,12,64]{0,2,1:T(8,128)(2,1)} %bitcast.126), kind=kOutput, calls=%fused_computation.4 | convolution fusion | flops 1673521152 | bytes 105693184 | tf_op jit(solution)/shard_map/qhd,khd->hqk/dot_general | solution.py:207
  1034.1 41.8 %multiply_convert_fusion.1 = bf16[12,512,2048]{2,1,0:T(8,128)(2,1)} fusion(f32[12,512,2048]{2,1,0:T(8,128)} %get-tuple-element.91, f32[12,512]{1,0:T(8,128)S(1)} %get-tuple-element.90, f32[12,512]{1,0:T(8,128)S(1)} %log_add_fusion.1, f32[12,512,2048]{2,1,0:T(8,128)} %get-tuple-element.86, pred[512,2048]{1,0:T(8,128)(4,1)} %get-tuple-element.72), kind=kLoop, calls=%fused_computation.3 | loop fusion | flops 75497472 | bytes 126926848 | tf_op jit(solution)/shard_map/convert_element_type | solution.py:211
  1075.9 13.7 multiply_bitcast_fusion.1
  1089.6 15.7 fusion.102
  1105.3 23.0 %fusion.5 = f32[12,64,2048]{2,1,0:T(8,128)} fusion(bf16[512,12,64]{0,2,1:T(8,128)(2,1)S(1)} %bitcast.142, f32[12,512]{1,0:T(8,128)S(1)} %log_add_fusion, f32[12,512,2048]{2,1,0:T(8,128)} %get-tuple-element.84, pred[512,2048]{1,0:T(8,128)(4,1)S(1)} %copy-done.5), kind=kOutput, calls=%fused_computation.16 | convolution fusion | flops 1660944384 | bytes 58482688 | tf_op jit(solution)/shard_map/hqk,qhd->khd/dot_general | solution.py:226
  1128.2 38.1 %multiply_reduce_fusion = (f32[12,512]{1,0:T(8,128)S(1)}, f32[12,512,2048]{2,1,0:T(8,128)}) fusion(f32[12,512]{1,0:T(8,128)S(1)} %log_add_fusion, f32[12,512,2048]{2,1,0:T(8,128)} %get-tuple-element.84, pred[512,2048]{1,0:T(8,128)(4,1)S(1)} %copy-done.5, bf16[512,12,64]{0,2,1:T(8,128)(2,1)} %bitcast.141, bf16[2048,12,64]{0,2,1:T(8,128)(2,1)} %bitcast.127), kind=kOutput, calls=%fused_computation.1 | convolution fusion | flops 1673521152 | bytes 105693184 | tf_op jit(solution)/shard_map/qhd,khd->hqk/dot_general | solution.py:207
  1166.3 25.4 %fusion.37 = f32[12,64,2048]{2,1,0:T(8,128)} fusion(f32[12,64,2048]{2,1,0:T(8,128)} %fusion.5, bf16[512,12,64]{0,2,1:T(8,128)(2,1)S(1)} %bitcast.140, f32[12,512]{1,0:T(8,128)S(1)} %log_add_fusion.1, f32[12,512,2048]{2,1,0:T(8,128)} %get-tuple-element.86, pred[512,2048]{1,0:T(8,128)(4,1)S(1)} %copy-done.8), kind=kOutput, calls=%fused_computation.76 | convolution fusion | flops 1662517248 | bytes 64774144 | tf_op jit(solution)/shard_map/hqk,qhd->khd/dot_general | solution.py:226
  1191.6 6.6 copy.62
  1198.2 40.4 %multiply_convert_fusion = bf16[12,512,2048]{2,1,0:T(8,128)(2,1)} fusion(f32[12,512,2048]{2,1,0:T(8,128)} %get-tuple-element.93, f32[12,512]{1,0:T(8,128)S(1)} %get-tuple-element.92, f32[12,512]{1,0:T(8,128)S(1)} %log_add_fusion, f32[12,512,2048]{2,1,0:T(8,128)} %get-tuple-element.84, pred[512,2048]{1,0:T(8,128)(4,1)S(1)} %copy-done.5), kind=kLoop, calls=%fused_computation | loop fusion | flops 75497472 | bytes 126926848 | tf_op jit(solution)/shard_map/convert_element_type | solution.py:211
  1238.6 17.1 add_multiply_fusion
  1255.7 6.6 copy.61
  1262.3 5.0 fusion.21
  1269.5 10.7 convolution_bitcast_fusion
  1285.8 9.7 copy.75
  1301.6 13.8 multiply_bitcast_fusion
  1324.3 4.2 fusion.20
  1330.6 4.8 fusion.16
  1335.5 5.6 fusion.18
  1342.5 13.7 multiply_reduce_fusion.4
  1356.3 8.5 fusion.58
  1364.8 5.7 fusion.45
  1370.7 5.7 fusion.96
  1395.7 4.9 constant_dynamic-update-slice_fusion.4
  1411.1 302.4 %fusion = f32[1744,128]{1,0:T(8,128)S(1)} fusion(f32[55392,128]{1,0:T(8,128)} %bitcast.31), kind=kCustom, calls=%all-reduce-scatter | all-reduce-scatter fusion | flops 7143425 | bytes 29253632
  1714.2 4.4 collective-permute-start.9
  1718.6 5.2 fusion.44
  1727.5 4.5 concatenate.77
  (256 shorter events, 133.6 us)
Async XLA Ops:
  7.2 919.4 %all-gather.3.cloned.1.call-start = ((), (), s32[]{:S(2)}) async-start(), calls=%async_computation | async-start | bytes 14665728 | tf_op jit(solution)/shard_map/all_gather | solution.py:170
  8.4 81.5 %copy-start.12 = (bf16[1731,128]{1,0:T(8,128)(2,1)}, bf16[1731,128]{1,0:T(8,128)(2,1)S(1)}, u32[]{:S(2)}) copy-start(bf16[1731,128]{1,0:T(8,128)(2,1)S(1)} %convert_element_type.133) | copy-start | bytes 1329412
  8.4 8.7 collective-permute-start
  17.1 72.8 %copy-start.14 = (bf16[1731,128]{1,0:T(8,128)(2,1)}, bf16[1731,128]{1,0:T(8,128)(2,1)S(1)}, u32[]{:S(2)}) copy-start(bf16[1731,128]{1,0:T(8,128)(2,1)S(1)} %collective-permute-done) | copy-start | bytes 1329412
  17.3 24.0 %collective-permute-start.1 = (bf16[3462,128]{1,0:T(8,128)(2,1)S(1)}, bf16[3462,128]{1,0:T(8,128)(2,1)S(1)}, u32[]{:S(2)}, u32[]{:S(2)}) collective-permute-start(bf16[3462,128]{1,0:T(8,128)(2,1)S(1)} %pad_maximum_fusion.7), channel_id=1, source_target_pairs={{0,30},{1,31},{2,0},{3,1},{4,2},{5,3},{6,4},{7,5},{8,6},{9,7},{10,... | collective-permute-start | bytes 2658824 | tf_op jit(solution)/shard_map/ppermute | solution.py:108
  41.2 48.7 %copy-start.11 = (bf16[3462,128]{1,0:T(8,128)(2,1)}, bf16[3462,128]{1,0:T(8,128)(2,1)S(1)}, u32[]{:S(2)}) copy-start(bf16[3462,128]{1,0:T(8,128)(2,1)S(1)} %collective-permute-done.1) | copy-start | bytes 2658820
  50.0 39.9 %collective-permute-start.2 = (bf16[6924,128]{1,0:T(8,128)(2,1)}, bf16[6924,128]{1,0:T(8,128)(2,1)S(1)}, u32[]{:S(2)}, u32[]{:S(2)}) collective-permute-start(bf16[6924,128]{1,0:T(8,128)(2,1)} %concatenate.61), channel_id=1, source_target_pairs={{0,28},{1,29},{2,30},{3,31},{4,0},{5,1},{6,2},{7,3},{8,4},{9,5},{1... | collective-permute-start | bytes 5317640 | tf_op jit(solution)/shard_map/ppermute | solution.py:108
  107.3 78.5 %collective-permute-start.3 = (bf16[13848,128]{1,0:T(8,128)(2,1)}, bf16[13848,128]{1,0:T(8,128)(2,1)S(1)}, u32[]{:S(2)}, u32[]{:S(2)}) collective-permute-start(bf16[13848,128]{1,0:T(8,128)(2,1)} %concatenate.62), channel_id=1, source_target_pairs={{0,24},{1,25},{2,26},{3,27},{4,28},{5,29},{6,30},{7,31},{8,0},{9,1... | collective-permute-start | bytes 10635272 | tf_op jit(solution)/shard_map/ppermute | solution.py:108
  215.7 7.6 copy-start.57
  215.7 316.3 %collective-permute-start.4 = (bf16[27696,128]{1,0:T(8,128)(2,1)}, bf16[27696,128]{1,0:T(8,128)(2,1)}, u32[]{:S(2)}, u32[]{:S(2)}) collective-permute-start(bf16[27696,128]{1,0:T(8,128)(2,1)} %concatenate.63), channel_id=1, source_target_pairs={{0,16},{1,17},{2,18},{3,19},{4,20},{5,21},{6,22},{7,23},{8,24},{9,... | collective-permute-start | bytes 21270536 | tf_op jit(solution)/shard_map/ppermute | solution.py:108
  226.4 463.8 %copy-start.46 = (f32[1024]{0:T(1024)}, f32[1024]{0:T(1024)S(1)}, u32[]{:S(2)}) copy-start(f32[1024]{0:T(1024)S(1)} %get-tuple-element.77) | copy-start | bytes 12292
  226.4 464.5 %copy-start.48 = (f32[1024]{0:T(1024)}, f32[1024]{0:T(1024)S(1)}, u32[]{:S(2)}) copy-start(f32[1024]{0:T(1024)S(1)} %get-tuple-element.78) | copy-start | bytes 12292
  652.5 15.0 copy-start.15
  652.5 15.0 copy-start.54
  673.6 3.4 collective-permute-start.5
  682.7 12.1 copy-start.52
  682.7 12.1 copy-start.60
  682.8 12.1 copy-start.61
  682.8 12.1 copy-start.62
  682.8 12.1 copy-start.63
  684.8 50.3 %collective-permute-start.6 = (bf16[1024,1536]{1,0:T(8,128)(2,1)S(1)}, bf16[1024,1536]{1,0:T(8,128)(2,1)}, u32[]{:S(2)}, u32[]{:S(2)}) collective-permute-start(bf16[1024,1536]{1,0:T(8,128)(2,1)S(1)} %slice.287), channel_id=1, source_target_pairs={{0,1},{1,2},{2,3},{4,5},{5,6},{6,7},{8,9},{9,10},{10,11},{12,13},{... | collective-permute-start | bytes 9437192 | tf_op jit(solution)/shard_map/ppermute | solution.py:17
  744.4 49.2 %copy-start.1 = (bf16[2048,768]{0,1:T(8,128)(2,1)}, bf16[2048,768]{0,1:T(8,128)(2,1)S(1)}, u32[]{:S(2)}) copy-start(bf16[2048,768]{0,1:T(8,128)(2,1)S(1)} %copy.56) | copy-start | bytes 9437188
  815.1 22.5 %copy-start.6 = (pred[512,2048]{1,0:T(8,128)(4,1)S(1)}, pred[512,2048]{1,0:T(8,128)(4,1)}, u32[]{:S(2)}) copy-start(pred[512,2048]{1,0:T(8,128)(4,1)} %get-tuple-element.72) | copy-start | bytes 3145732
  815.1 22.6 %copy-start.10 = (bf16[2048,768]{0,1:T(8,128)(2,1)S(1)}, bf16[2048,768]{0,1:T(8,128)(2,1)}, u32[]{:S(2)}) copy-start(bf16[2048,768]{0,1:T(8,128)(2,1)} %copy.54) | copy-start | bytes 9437188
  837.7 21.1 %copy-start.4 = (pred[512,2048]{1,0:T(8,128)(4,1)S(1)}, pred[512,2048]{1,0:T(8,128)(4,1)}, u32[]{:S(2)}) copy-start(pred[512,2048]{1,0:T(8,128)(4,1)} %get-tuple-element.73) | copy-start | bytes 3145732
  858.7 21.3 %copy-start.16 = (bf16[1024,768]{0,1:T(8,128)(2,1)S(1)}, bf16[1024,768]{0,1:T(8,128)(2,1)}, u32[]{:S(2)}) copy-start(bf16[1024,768]{0,1:T(8,128)(2,1)} %copy.53) | copy-start | bytes 4718596
  858.7 21.3 %copy-start.39 = (bf16[768,768]{1,0:T(8,128)(2,1)S(1)}, bf16[768,768]{1,0:T(8,128)(2,1)}, u32[]{:S(2)}) copy-start(bf16[768,768]{1,0:T(8,128)(2,1)} %reshape.388) | copy-start | bytes 3538948
  883.2 109.7 %copy-start.20 = (f32[1024,768]{0,1:T(8,128)}, f32[1024,768]{0,1:T(8,128)S(1)}, u32[]{:S(2)}) copy-start(f32[1024,768]{0,1:T(8,128)S(1)} %get-tuple-element.88) | copy-start | bytes 9437188
  883.3 109.7 %copy-start.42 = (f32[1024]{0:T(1024)}, f32[1024]{0:T(1024)S(1)}, u32[]{:S(2)}) copy-start(f32[1024]{0:T(1024)S(1)} %add_rsqrt_fusion) | copy-start | bytes 12292
  893.4 11.7 copy-start.56
  983.0 9.9 copy-start.69
  983.0 9.9 copy-start.28
  996.7 37.5 %copy-start.33 = (bf16[512,768]{0,1:T(8,128)(2,1)}, bf16[512,768]{0,1:T(8,128)(2,1)S(1)}, u32[]{:S(2)}) copy-start(bf16[512,768]{0,1:T(8,128)(2,1)S(1)} %get-tuple-element.62) | copy-start | bytes 2359300
  1034.1 41.8 %copy-start.2 = (bf16[2048,768]{0,1:T(8,128)(2,1)S(1)}, bf16[2048,768]{0,1:T(8,128)(2,1)}, u32[]{:S(2)}) copy-start(bf16[2048,768]{0,1:T(8,128)(2,1)} %copy-done.1) | copy-start | bytes 9437188
  1089.6 15.7 copy-start.5
  1089.6 15.7 copy-start.35
  1128.2 38.1 %copy-start.8 = (pred[512,2048]{1,0:T(8,128)(4,1)S(1)}, pred[512,2048]{1,0:T(8,128)(4,1)}, u32[]{:S(2)}) copy-start(pred[512,2048]{1,0:T(8,128)(4,1)} %get-tuple-element.72) | copy-start | bytes 3145732
  1128.2 38.1 %copy-start.34 = (bf16[512,768]{0,1:T(8,128)(2,1)S(1)}, bf16[512,768]{0,1:T(8,128)(2,1)}, u32[]{:S(2)}) copy-start(bf16[512,768]{0,1:T(8,128)(2,1)} %copy-done.33) | copy-start | bytes 2359300
  1198.2 40.4 %copy-start.26 = (bf16[512,768]{0,1:T(8,128)(2,1)S(1)}, bf16[512,768]{0,1:T(8,128)(2,1)}, u32[]{:S(2)}) copy-start(bf16[512,768]{0,1:T(8,128)(2,1)} %copy.57) | copy-start | bytes 2359300
  1267.3 12.9 copy-start.32
  1267.3 14.7 copy-start.31
  1267.3 16.6 copy-start.30
  1267.3 57.0 %collective-permute-start.7 = (bf16[1024,1536]{1,0:T(8,128)(2,1)}, bf16[1024,1536]{1,0:T(8,128)(2,1)}, u32[]{:S(2)}, u32[]{:S(2)}) collective-permute-start(bf16[1024,1536]{1,0:T(8,128)(2,1)} %fusion.21), channel_id=1, source_target_pairs={{1,0},{2,1},{3,2},{5,4},{6,5},{7,6},{9,8},{10,9},{11,10},{13,12},{... | collective-permute-start | bytes 9437192 | tf_op jit(solution)/shard_map/ppermute | solution.py:17
  1285.8 9.7 copy-start.23
  1285.8 9.7 copy-start.67
  1285.8 9.7 copy-start.68
  1328.7 12.4 collective-permute-start.8
  1342.4 13.8 copy-start.17
  1342.4 13.8 copy-start.55
  1342.5 13.8 copy-start.65
  1356.2 8.6 copy-start.29
  1356.3 8.6 copy-start.36
  1356.3 8.5 copy-start.37
  1356.3 8.5 copy-start.38
  1356.3 8.5 copy-start.53
  1382.8 12.2 slice-start.6
  1384.4 9.0 copy-start.24
  1384.4 10.6 slice-start.7
  1411.1 307.5 %copy-start.18 = (bf16[1024,768]{0,1:T(8,128)(2,1)S(1)}, bf16[1024,768]{0,1:T(8,128)(2,1)}, u32[]{:S(2)}) copy-start(bf16[1024,768]{0,1:T(8,128)(2,1)} %copy.53) | copy-start | bytes 4718596
  1714.2 13.3 collective-permute-start.9
  1723.8 8.2 copy-start.27
  1723.8 8.2 copy-start.41
  1723.8 8.2 copy-start.50
  1723.8 8.2 copy-start.51
  (28 other events, 136.7 us)
Sparse Core Ops, SparseCore 0:
  217.8 393.6 all-gather.2
